TPU v7x, 32 devices: a whole 2x2x4 slice. The times are simulated.
32 devices in a mesh: occ: 4 (over z), va: 2 (over x), vb: 4 (over y, core).
Axes of the slice: x: 2, y: 2, z: 4, core: 2. Of those that a mesh axis runs over, the one named last changes fastest.
Arguments:
- aux_factors: bfloat16 [4, 1024, 2048], P('occ', ('vb', 'va')), may hold values from -0.59765625 to 0.59765625
- occ_energy: float32 [4], replicated, may hold values from -2 to -0.5
- vir_energy: float32 [1024], replicated, may hold values from 0.5 to 3
- occ_index: int32 [4], replicated, may hold values from 0 to 3, each once
- vir_index: int32 [1024], replicated, may hold values from 0 to 1023, each once
Outputs:
- gamma_aux: float32 [4, 1024, 2048], P('occ', ('vb', 'va'))
Inputs may be any that keep to these rules, and one draw needn't show every extreme that they name: `occ_index`: each occupied table row appears exactly once. `vir_index`: each virtual table row appears exactly once.
All inputs are finite; a program needn't handle non-finite values.
Results may differ from a plain program's by a relative error of at most 0.0017.
Values may be sent and summed in bfloat16 or wider, within the bound.
No kernel may reach another device: no remote copies, remote signals or barrier semaphores. Data moves between devices by JAX's collectives and lax.ppermute only.
A program may use at most 64 MiB of HBM per device.

v0:
```python
import jax
import jax.numpy as jnp
from jax import lax
from jax.sharding import PartitionSpec as P

STEPS = 4


def passed_along(block, axis, distance):
    devices = range(lax.axis_size(axis))
    route = [((i - distance) % len(devices), i) for i in devices]
    return lax.ppermute(block, axis, route)


def lookup(indices, energies):
    positions = jnp.arange(energies.shape[0], dtype=jnp.int32)
    matches = indices[:, None] == positions[None, :]
    return jnp.sum(jnp.where(matches, energies[None, :], 0.0), axis=1)


def per_device(aux_factors, occ_energy, vir_energy, occ_index, vir_index):
    va_count = lax.axis_size("va")
    vb_count = lax.axis_size("vb")
    occ_count = lax.axis_size("occ")
    va_rank = lax.axis_index("va")
    vb_rank = lax.axis_index("vb")
    occ_rank = lax.axis_index("occ")
    occ_rows, block_width, aux_width = aux_factors.shape
    vir_width = vir_index.shape[0]
    row_count = vb_count * block_width
    col_count = va_count * block_width
    row_index = lax.dynamic_index_in_dim(
        vir_index.reshape(vb_count, va_count, block_width), va_rank, 1, False
    ).reshape(row_count)
    col_index = lax.dynamic_index_in_dim(
        vir_index.reshape(vb_count, vir_width // vb_count), vb_rank, 0, False
    )
    row_energy = lookup(row_index, vir_energy)
    col_energy = lookup(col_index, vir_energy)

    def block_energy(block_id):
        return lookup(
            lax.dynamic_slice_in_dim(occ_index, block_id * occ_rows, occ_rows), occ_energy
        )

    own_energy = block_energy(occ_rank)
    own_columns = lax.all_gather(aux_factors, "va", axis=1, tiled=True)
    own_rows = lax.all_gather(aux_factors, "vb", axis=1, tiled=True)
    gradient = jnp.zeros((occ_rows, row_count, aux_width), jnp.float32)
    far_columns = own_columns
    for distance in range(STEPS):
        if distance > 0:
            far_columns = passed_along(far_columns, "occ", 1)
        far_block = (occ_rank - distance + occ_count) % occ_count
        kernel = jnp.einsum(
            "iap,jbp->iajb", own_rows, far_columns, preferred_element_type=jnp.float32
        )
        outgoing = kernel.reshape(occ_rows, vb_count, block_width, occ_rows, va_count, block_width)
        outgoing = outgoing.transpose(4, 1, 0, 2, 3, 5).reshape(
            va_count * vb_count, occ_rows, block_width, occ_rows, block_width
        )
        incoming = lax.all_to_all(outgoing, ("va", "vb"), split_axis=0, concat_axis=0, tiled=True)
        incoming = incoming.reshape(
            va_count, vb_count, occ_rows, block_width, occ_rows, block_width
        )
        swapped = incoming.transpose(2, 1, 5, 4, 0, 3).reshape(
            occ_rows, row_count, occ_rows, col_count
        )
        energy_gap = (
            own_energy[:, None, None, None]
            + block_energy(far_block)[None, None, :, None]
            - row_energy[None, :, None, None]
            - col_energy[None, None, None, :]
        )
        weights = ((2.0 * kernel - swapped) / energy_gap).astype(jnp.bfloat16)
        gradient = gradient + jnp.einsum(
            "iajb,jbp->iap", weights, far_columns, preferred_element_type=jnp.float32
        )
    return lax.psum_scatter(gradient, "vb", scatter_dimension=1, tiled=True)


def solution(mesh):
    return jax.shard_map(
        per_device,
        mesh=mesh,
        in_specs=(P("occ", ("vb", "va"), None), P(), P(), P(), P()),
        out_specs=P("occ", ("vb", "va"), None),
        check_vma=False,
    )
```

profile of v0, /device:TPU:0, one launch (start us, length us, event | category | flops | bytes accessed | tf_op | source)
XLA Modules:
  0.0 195.6 jit_solution(13095508665357366006)
XLA Ops:
  6.5 0.7 all-gather.5.cloned.1.call-update
  7.3 0.0 all-gather.3.cloned.1.call-start
  7.3 0.7 all-gather.3.cloned.1.call-update
  8.0 24.9 %all-gather.5.cloned.1.call-done = bf16[1,256,2048]{2,1,0:T(8,128)(2,1)} async-done(((bf16[1,128,2048]{2,1,0:T(8,128)(2,1)}), bf16[1,256,2048]{2,1,0:T(8,128)(2,1)}) %all-gather.5.cloned.1.call-update) | async-done | bytes 1048592 | tf_op jit(solution)/shard_map/all_gather | solution.py:47
  32.9 1.5 collective-permute-start
  34.4 25.3 %collective-permute-done = bf16[1,256,2048]{2,1,0:T(8,128)(2,1)S(1)} collective-permute-done((bf16[1,256,2048]{2,1,0:T(8,128)(2,1)}, bf16[1,256,2048]{2,1,0:T(8,128)(2,1)S(1)}, u32[]{:S(2)}, u32[]{:S(2)}) %collective-permute-start) | collective-permute-done | bytes 1048608 | tf_op jit(solution)/shard_map/ppermute | solution.py:12
  59.7 0.0 collective-permute-start.1
  59.7 1.6 fusion.52
  61.2 4.4 %fusion.47 = (f32[]{:T(128)}, f32[]{:T(128)}, f32[]{:T(128)}, f32[]{:T(128)}, f32[]{:T(128)}) fusion(f32[4]{0:T(128)} %param.6, s32[]{:T(128)} %bitcast.32, s32[]{:T(128)} %bitcast.18, s32[]{:T(128)} %bitcast.8, s32[]{:T(128)} %bitcast.7, s32[]{:T(128)} %bitcast.25), kind=kLoop, calls=%fused_computation.61 | loop fusion | flops 55 | bytes 56 | tf_op jit(solution)/shard_map/reduce_sum | solution.py:18
  70.6 0.7 reshape.218
  71.3 0.7 constant_dynamic-slice_fusion.1
  72.0 1.0 select_reduce_fusion
  73.1 12.3 %collective-permute-done.1 = bf16[1,256,2048]{2,1,0:T(8,128)(2,1)S(1)} collective-permute-done((bf16[1,256,2048]{2,1,0:T(8,128)(2,1)S(1)}, bf16[1,256,2048]{2,1,0:T(8,128)(2,1)S(1)}, u32[]{:S(2)}, u32[]{:S(2)}) %collective-permute-start.1) | collective-permute-done | bytes 1048608 | tf_op jit(solution)/shard_map/ppermute | solution.py:12
  85.3 2.7 %fusion.2 = f32[512,256]{1,0:T(8,128)S(1)} fusion(bf16[1,512,2048]{2,1,0:T(8,128)(2,1)} %all-gather.3.cloned.1.call-done, bf16[1,256,2048]{2,1,0:T(8,128)(2,1)S(1)} %collective-permute-done.1), kind=kOutput, calls=%fused_computation.3 | convolution fusion | flops 536870912 | bytes 3670016 | tf_op jit(solution)/shard_map/iap,jbp->iajb/dot_general | solution.py:55
  88.1 0.3 reshape.225
  88.3 0.8 copy.32
  89.2 3.5 %all-to-all-start.2 = ((f32[8,1,128,1,128]{4,2,3,1,0:T(8,128)}), f32[8,1,128,1,128]{4,2,3,1,0:T(8,128)S(1)}, u32[]{:S(2)}, u32[]{:S(2)}) async-start(f32[8,1,128,1,128]{4,2,3,1,0:T(8,128)} %bitcast.22), calls=%async_computation.2 | async-start | bytes 1048576 | tf_op jit(solution)/shard_map/all_to_all | solution.py:62
  92.7 0.1 collective-permute-start.2
  92.8 2.3 %fusion.4 = f32[512,256]{1,0:T(8,128)S(1)} fusion(bf16[1,512,2048]{2,1,0:T(8,128)(2,1)} %all-gather.3.cloned.1.call-done, bf16[1,256,2048]{2,1,0:T(8,128)(2,1)S(1)} %collective-permute-done), kind=kOutput, calls=%fused_computation.5 | convolution fusion | flops 536870912 | bytes 3670016 | tf_op jit(solution)/shard_map/iap,jbp->iajb/dot_general | solution.py:55
  95.1 0.0 copy-start.2
  95.1 0.3 reshape.220
  95.4 0.8 copy.29
  96.2 5.2 %all-to-all-done.2 = f32[8,1,128,1,128]{4,2,3,1,0:T(8,128)S(1)} async-done(((f32[8,1,128,1,128]{4,2,3,1,0:T(8,128)}), f32[8,1,128,1,128]{4,2,3,1,0:T(8,128)S(1)}, u32[]{:S(2)}, u32[]{:S(2)}) %all-to-all-start.2) | async-done | bytes 524320 | tf_op jit(solution)/shard_map/all_to_all | solution.py:62
  101.5 3.5 %all-to-all-start.1 = ((f32[8,1,128,1,128]{4,2,3,1,0:T(8,128)}), f32[8,1,128,1,128]{4,2,3,1,0:T(8,128)S(1)}, u32[]{:S(2)}, u32[]{:S(2)}) async-start(f32[8,1,128,1,128]{4,2,3,1,0:T(8,128)} %bitcast.15), calls=%async_computation.1 | async-start | bytes 1048576 | tf_op jit(solution)/shard_map/all_to_all | solution.py:62
  105.0 0.2 select_reduce_fusion.1
  105.2 2.6 %fusion.6 = f32[512,256]{1,0:T(8,128)S(1)} fusion(bf16[1,512,2048]{2,1,0:T(8,128)(2,1)} %all-gather.3.cloned.1.call-done, bf16[1,256,2048]{2,1,0:T(8,128)(2,1)} %all-gather.5.cloned.1.call-done), kind=kOutput, calls=%fused_computation.7 | convolution fusion | flops 536870912 | bytes 3670016 | tf_op jit(solution)/shard_map/iap,jbp->iajb/dot_general | solution.py:55
  107.8 0.3 reshape.213
  108.1 0.8 copy.26
  109.0 0.3 copy.34
  109.2 4.5 %all-to-all-done.1 = f32[8,1,128,1,128]{4,2,3,1,0:T(8,128)S(1)} async-done(((f32[8,1,128,1,128]{4,2,3,1,0:T(8,128)}), f32[8,1,128,1,128]{4,2,3,1,0:T(8,128)S(1)}, u32[]{:S(2)}, u32[]{:S(2)}) %all-to-all-start.1) | async-done | bytes 524320 | tf_op jit(solution)/shard_map/all_to_all | solution.py:62
  113.7 3.5 %all-to-all-start = ((f32[8,1,128,1,128]{4,2,3,1,0:T(8,128)}), f32[8,1,128,1,128]{4,2,3,1,0:T(8,128)S(1)}, u32[]{:S(2)}, u32[]{:S(2)}) async-start(f32[8,1,128,1,128]{4,2,3,1,0:T(8,128)} %bitcast.118), calls=%async_computation | async-start | bytes 1048576 | tf_op jit(solution)/shard_map/all_to_all | solution.py:62
  117.2 3.9 %fusion.10 = f32[512,2048]{1,0:T(8,128)} fusion(bf16[1,256,2048]{2,1,0:T(8,128)(2,1)} %copy-done.1, f32[64,8,2,128]{3,2,1,0:T(2,128)S(1)} %bitcast.112, f32[512,256]{1,0:T(8,128)S(1)} %fusion.2, f32[512]{0:T(512)S(1)} %get-tuple-element.11, f32[256]{0:T(256)S(1)} %select_reduce_fusion.1), kind=kOutput, calls=%fused_computation.13 | convolution fusion | flops 537526272 | bytes 6294528 | tf_op jit(solution)/shard_map/iajb,jbp->iap/dot_general | solution.py:76
  121.2 0.3 copy.31
  121.4 0.0 collective-permute-done.2
  121.4 2.6 %fusion = f32[512,256]{1,0:T(8,128)S(1)} fusion(bf16[1,512,2048]{2,1,0:T(8,128)(2,1)} %all-gather.3.cloned.1.call-done, bf16[1,256,2048]{2,1,0:T(8,128)(2,1)} %collective-permute-done.2), kind=kOutput, calls=%fused_computation.1 | convolution fusion | flops 536870912 | bytes 3670016 | tf_op jit(solution)/shard_map/iap,jbp->iajb/dot_general | solution.py:55
  124.0 0.3 reshape.230
  124.3 0.8 copy.35
  125.1 0.9 all-to-all-done
  126.0 3.5 %all-to-all-start.3 = ((f32[8,1,128,1,128]{4,2,3,1,0:T(8,128)}), f32[8,1,128,1,128]{4,2,3,1,0:T(8,128)S(1)}, u32[]{:S(2)}, u32[]{:S(2)}) async-start(f32[8,1,128,1,128]{4,2,3,1,0:T(8,128)} %bitcast.29), calls=%async_computation.3 | async-start | bytes 1048576 | tf_op jit(solution)/shard_map/all_to_all | solution.py:62
  129.5 0.0 reduce-scatter.2.cloned.1.call-start
  129.6 4.0 %fusion.13 = f32[512,2048]{1,0:T(8,128)} fusion(bf16[1,256,2048]{2,1,0:T(8,128)(2,1)} %copy-done, f32[64,8,2,128]{3,2,1,0:T(2,128)S(1)} %bitcast.111, f32[512,256]{1,0:T(8,128)S(1)} %fusion.4, f32[512]{0:T(512)S(1)} %get-tuple-element.12, f32[256]{0:T(256)S(1)} %select_reduce_fusion.1), kind=kOutput, calls=%fused_computation.16 | convolution fusion | flops 537526272 | bytes 6294528 | tf_op jit(solution)/shard_map/iajb,jbp->iap/dot_general | solution.py:76
  133.6 0.3 copy.28
  133.8 4.0 %fusion.16 = f32[512,2048]{1,0:T(8,128)} fusion(bf16[1,256,2048]{2,1,0:T(8,128)(2,1)} %all-gather.5.cloned.1.call-done, f32[64,8,2,128]{3,2,1,0:T(2,128)S(1)} %bitcast.114, f32[512,256]{1,0:T(8,128)S(1)} %fusion.6, f32[256]{0:T(256)S(1)} %select_reduce_fusion.1, f32[512]{0:T(512)S(1)} %get-tuple-element.13), kind=kOutput, calls=%fused_computation.19 | convolution fusion | flops 537526272 | bytes 6294528 | tf_op jit(solution)/shard_map/iajb,jbp->iap/dot_general | solution.py:76
  137.8 0.5 all-to-all-done.3
  138.3 0.3 copy.37
  138.6 7.8 %add_bitcast_fusion = f32[1,512,2048]{2,1,0:T(8,128)} fusion(f32[512,2048]{1,0:T(8,128)} %fusion.10, f32[512,2048]{1,0:T(8,128)} %fusion.16, f32[512,2048]{1,0:T(8,128)} %fusion.13, bf16[1,256,2048]{2,1,0:T(8,128)(2,1)} %collective-permute-done.2, f32[64,8,2,128]{3,2,1,0:T(2,128)S(1)} %bitcast.113, f32[512,256]{1,0:T(8,128)S(1)} %fusion, ...), kind=kOutput, calls=%fused_computation | convolution fusion | flops 540672000 | bytes 18877440 | tf_op jit(solution)/shard_map/iajb,jbp->iap/dot_general | solution.py:76
  146.3 0.0 reduce-scatter.2.cloned.1.call-update
  146.4 42.8 %reduce-scatter.2.cloned.1.call-done = f32[1,128,2048]{2,1,0:T(8,128)} async-done(((f32[1,512,2048]{2,1,0:T(8,128)}), f32[1,128,2048]{2,1,0:T(8,128)}) %reduce-scatter.2.cloned.1.call-update) | async-done | bytes 1048592 | tf_op jit(solution)/shard_map/reduce_scatter | solution.py:79
  (9 shorter events, 0.0 us)
Async XLA Ops:
  6.5 26.4 %all-gather.5.cloned.1.call-start = ((), (), s32[]{:S(2)}) async-start(), calls=%async_computation.6 | async-start | bytes 1572864 | tf_op jit(solution)/shard_map/all_gather | solution.py:47
  7.3 78.1 %all-gather.3.cloned.1.call-start = ((), (), s32[]{:S(2)}) async-start(), calls=%async_computation.5 | async-start | bytes 2621440 | tf_op jit(solution)/shard_map/all_gather | solution.py:48
  32.9 26.7 %collective-permute-start = (bf16[1,256,2048]{2,1,0:T(8,128)(2,1)}, bf16[1,256,2048]{2,1,0:T(8,128)(2,1)S(1)}, u32[]{:S(2)}, u32[]{:S(2)}) collective-permute-start(bf16[1,256,2048]{2,1,0:T(8,128)(2,1)} %all-gather.5.cloned.1.call-done), channel_id=1, source_target_pairs={{24,0},{0,8},{8,16},{16,24},{25,1},{1,9},{9,17},{17,25},{26,2},{2,... | collective-permute-start | bytes 3145736 | tf_op jit(solution)/shard_map/ppermute | solution.py:12
  59.7 33.1 %copy-start = (bf16[1,256,2048]{2,1,0:T(8,128)(2,1)}, bf16[1,256,2048]{2,1,0:T(8,128)(2,1)S(1)}, u32[]{:S(2)}) copy-start(bf16[1,256,2048]{2,1,0:T(8,128)(2,1)S(1)} %collective-permute-done) | copy-start | bytes 3145732
  59.7 25.7 %collective-permute-start.1 = (bf16[1,256,2048]{2,1,0:T(8,128)(2,1)S(1)}, bf16[1,256,2048]{2,1,0:T(8,128)(2,1)S(1)}, u32[]{:S(2)}, u32[]{:S(2)}) collective-permute-start(bf16[1,256,2048]{2,1,0:T(8,128)(2,1)S(1)} %collective-permute-done), channel_id=1, source_target_pairs={{24,0},{0,8},{8,16},{16,24},{25,1},{1,9},{9,17},{17,25},{26,2},{2,... | collective-permute-start | bytes 3145736 | tf_op jit(solution)/shard_map/ppermute | solution.py:12
  85.3 2.7 %copy-start.1 = (bf16[1,256,2048]{2,1,0:T(8,128)(2,1)}, bf16[1,256,2048]{2,1,0:T(8,128)(2,1)S(1)}, u32[]{:S(2)}) copy-start(bf16[1,256,2048]{2,1,0:T(8,128)(2,1)S(1)} %collective-permute-done.1) | copy-start | bytes 3145732
  89.2 12.3 %all-to-all-start.2 = ((f32[8,1,128,1,128]{4,2,3,1,0:T(8,128)}), f32[8,1,128,1,128]{4,2,3,1,0:T(8,128)S(1)}, u32[]{:S(2)}, u32[]{:S(2)}) async-start(f32[8,1,128,1,128]{4,2,3,1,0:T(8,128)} %bitcast.22), calls=%async_computation.2 | async-start | bytes 1048576 | tf_op jit(solution)/shard_map/all_to_all | solution.py:62
  92.7 28.7 %collective-permute-start.2 = (bf16[1,256,2048]{2,1,0:T(8,128)(2,1)}, bf16[1,256,2048]{2,1,0:T(8,128)(2,1)}, u32[]{:S(2)}, u32[]{:S(2)}) collective-permute-start(bf16[1,256,2048]{2,1,0:T(8,128)(2,1)} %copy-done.1), channel_id=1, source_target_pairs={{24,0},{0,8},{8,16},{16,24},{25,1},{1,9},{9,17},{17,25},{26,2},{2,... | collective-permute-start | bytes 3145736 | tf_op jit(solution)/shard_map/ppermute | solution.py:12
  95.1 9.9 %copy-start.2 = (f32[1024]{0:T(1024)S(1)}, f32[1024]{0:T(1024)}, u32[]{:S(2)}) copy-start(f32[1024]{0:T(1024)} %param.7) | copy-start | bytes 12292
  101.5 12.3 %all-to-all-start.1 = ((f32[8,1,128,1,128]{4,2,3,1,0:T(8,128)}), f32[8,1,128,1,128]{4,2,3,1,0:T(8,128)S(1)}, u32[]{:S(2)}, u32[]{:S(2)}) async-start(f32[8,1,128,1,128]{4,2,3,1,0:T(8,128)} %bitcast.15), calls=%async_computation.1 | async-start | bytes 1048576 | tf_op jit(solution)/shard_map/all_to_all | solution.py:62
  113.7 12.3 %all-to-all-start = ((f32[8,1,128,1,128]{4,2,3,1,0:T(8,128)}), f32[8,1,128,1,128]{4,2,3,1,0:T(8,128)S(1)}, u32[]{:S(2)}, u32[]{:S(2)}) async-start(f32[8,1,128,1,128]{4,2,3,1,0:T(8,128)} %bitcast.118), calls=%async_computation | async-start | bytes 1048576 | tf_op jit(solution)/shard_map/all_to_all | solution.py:62
  126.0 12.3 %all-to-all-start.3 = ((f32[8,1,128,1,128]{4,2,3,1,0:T(8,128)}), f32[8,1,128,1,128]{4,2,3,1,0:T(8,128)S(1)}, u32[]{:S(2)}, u32[]{:S(2)}) async-start(f32[8,1,128,1,128]{4,2,3,1,0:T(8,128)} %bitcast.29), calls=%async_computation.3 | async-start | bytes 1048576 | tf_op jit(solution)/shard_map/all_to_all | solution.py:62
  129.5 59.6 %reduce-scatter.2.cloned.1.call-start = ((), (), s32[]{:S(2)}) async-start(), calls=%async_computation.7 | async-start | bytes 5242880 | tf_op jit(solution)/shard_map/reduce_scatter | solution.py:79
Sparse Core Ops, SparseCore 0:
  8.9 23.9 all-gather.4
  34.5 22.5 all-gather.2
  146.5 42.5 reduce-scatter.1
where the time goes:
time: 197 us; the launch traced here: 196 us
  waiting for transfers between devices  118 us (60%)
  matrix products  29.9 us (15%)
  between operations  18.3 us (9%)
  starting transfers between devices  15.6 us (8%)
  local copies, waits for them, and re-layouts  8.41 us (4%)
  other arithmetic  5.74 us (3%)
    reduce_scatter x1, waiting for transfers between devices, per_device(): return lax.psum_scatter(gradient, 'vb', scatter_dimension=1, tiled=True)  42.8 us
    ppermute x3, waiting for transfers between devices, passed_along(): return lax.ppermute(block, axis, route)  37.5 us
    all_gather x1, waiting for transfers between devices, per_device(): own_columns = lax.all_gather(aux_factors, 'va', axis=1, tiled=True)  24.9 us
    dot_general x4, matrix products, per_device(): jnp.einsum('iajb,jbp->iap', weights, far_columns, preferred_element_type=...  19.6 us
    all_to_all x4, starting transfers between devices, per_device(): lax.all_to_all(outgoing, ('va', 'vb'), split_axis=0, concat_axis=0, tiled...  14 us
    all_to_all x4, waiting for transfers between devices, per_device(): lax.all_to_all(outgoing, ('va', 'vb'), split_axis=0, concat_axis=0, tiled...  11.1 us
    dot_general x4, matrix products, per_device(): jnp.einsum('iap,jbp->iajb', own_rows, far_columns, preferred_element_type...  10.2 us
    reduce_sum x3, other arithmetic, lookup(): return jnp.sum(jnp.where(matches, energies[None, :], 0.0), axis=1)  5.73 us
  transfers between devices with their start and end apart: 10, of which 8 were waited for; matrix products, arithmetic and copies ran while one was open for 16% of the time, Pallas kernels for 0%

commit v1 on v0

--- a/solution.py
+++ b/solution.py
@@ -4,6 +4,14 @@
 from jax.sharding import PartitionSpec as P
 
 STEPS = 4
+
+
+def _serve_rings(mesh_ax, work_x, pos_dim):
+    carry_in = lax.axis_size(mesh_ax)
+    opened = jnp.stack(carry_in * [work_x], axis=0)
+    r_now = lax.all_to_all(opened, axis_name=mesh_ax, split_axis=0, concat_axis=0)
+    mat_out = jnp.concatenate(r_now, axis=pos_dim)
+    return mat_out
 
 
 def passed_along(block, axis, distance):
@@ -44,7 +52,7 @@
         )
 
     own_energy = block_energy(occ_rank)
-    own_columns = lax.all_gather(aux_factors, "va", axis=1, tiled=True)
+    own_columns = _serve_rings("va", aux_factors, 1)
     own_rows = lax.all_gather(aux_factors, "vb", axis=1, tiled=True)
     gradient = jnp.zeros((occ_rows, row_count, aux_width), jnp.float32)
     far_columns = own_columns

time: 197 us -> 184 us (0.934)
  waiting for transfers between devices: 118 us -> 83 us
  blocking collectives: 0 us -> 17.6 us
  local copies, waits for them, and re-layouts: 8.41 us -> 11.8 us
    all_gather x1 -> x0, waiting for transfers between devices: 24.9 us -> none  [per_device(): own_columns = lax.all_gather(aux_factors, 'va', axis=1, tiled=True)]
    all_to_all x0 -> x1, blocking collectives: none -> 17.6 us  [_serve_rings(): lax.all_to_all(opened, axis_name=mesh_ax, split_axis=0, concat_axis=0)]
    all_to_all x4, waiting for transfers between devices: 11.1 us -> 2.74 us  [per_device(): lax.all_to_all(outgoing, ('va', 'vb'), split_axis=0, concat_axis=0, tiled...]
    ppermute x3, waiting for transfers between devices: 37.5 us -> 33 us  [passed_along(): return lax.ppermute(block, axis, route)]
    reduce_scatter x1, waiting for transfers between devices: 42.8 us -> 46.5 us  [per_device(): return lax.psum_scatter(gradient, 'vb', scatter_dimension=1, tiled=True)]
    transpose x4, local copies, waits for them, and re-layouts: 1.01 us -> 4.48 us  [per_device(): incoming.transpose(2, 1, 5, 4, 0, 3)]
    reshape x8, local copies, waits for them, and re-layouts: 4.43 us -> 6.66 us  [per_device(): kernel.reshape(occ_rows, vb_count, block_width, occ_rows, va_count, block...]
  transfers between devices with their start and end apart: 10 -> 9, of which waited for: 8 -> 5; matrix products, arithmetic and copies ran while one was open for 16% -> 21% of each run, Pallas kernels for 0% -> 0%
where the time goes in v1:
time: 184 us; the launch traced here: 183 us
  waiting for transfers between devices  83 us (45%)
  matrix products  28.6 us (16%)
  between operations  18.7 us (10%)
  blocking collectives  17.6 us (10%)
  starting transfers between devices  17.1 us (9%)
  local copies, waits for them, and re-layouts  11.8 us (6%)
  other arithmetic  5.73 us (3%)
    reduce_scatter x1, waiting for transfers between devices, per_device(): return lax.psum_scatter(gradient, 'vb', scatter_dimension=1, tiled=True)  46.5 us
    ppermute x3, waiting for transfers between devices, passed_along(): return lax.ppermute(block, axis, route)  33 us
    dot_general x4, matrix products, per_device(): jnp.einsum('iajb,jbp->iap', weights, far_columns, preferred_element_type=...  18.8 us
    all_to_all x1, blocking collectives, _serve_rings(): lax.all_to_all(opened, axis_name=mesh_ax, split_axis=0, concat_axis=0)  17.6 us
    all_to_all x4, starting transfers between devices, per_device(): lax.all_to_all(outgoing, ('va', 'vb'), split_axis=0, concat_axis=0, tiled...  15.3 us
    dot_general x4, matrix products, per_device(): jnp.einsum('iap,jbp->iajb', own_rows, far_columns, preferred_element_type...  9.77 us
    reshape x8, local copies, waits for them, and re-layouts, per_device(): kernel.reshape(occ_rows, vb_count, block_width, occ_rows, va_count, block...  6.66 us
    transpose x4, local copies, waits for them, and re-layouts, per_device(): incoming.transpose(2, 1, 5, 4, 0, 3)  4.48 us
  transfers between devices with their start and end apart: 9, of which 5 were waited for; matrix products, arithmetic and copies ran while one was open for 21% of the time, Pallas kernels for 0%

profile of v1, /device:TPU:0, one launch (start us, length us, event | category | flops | bytes accessed | tf_op | source)
XLA Modules:
  0.0 182.6 jit_solution(5890638022721219750)
XLA Ops:
  6.5 0.0 all-gather.2.cloned.1.call-start
  6.6 0.7 all-gather.2.cloned.1.call-update
  7.3 1.4 pad_maximum_fusion
  8.7 17.6 %all_to_all.25 = bf16[2,1,128,2048]{3,2,1,0:T(8,128)(2,1)S(1)} all-to-all(bf16[2,1,128,2048]{3,2,1,0:T(8,128)(2,1)S(1)} %pad_maximum_fusion), channel_id=1, replica_groups=mesh['occ'=4,'va'=2,'vb'=4] {'va'}, dimensions={0} | all-to-all | bytes 2097152 | tf_op jit(solution)/shard_map/all_to_all | solution.py:12
  26.3 1.8 collective-permute-start
  28.0 24.4 %collective-permute-done = bf16[1,256,2048]{2,1,0:T(8,128)(2,1)} collective-permute-done((bf16[1,256,2048]{2,1,0:T(8,128)(2,1)S(1)}, bf16[1,256,2048]{2,1,0:T(8,128)(2,1)}, u32[]{:S(2)}, u32[]{:S(2)}) %collective-permute-start) | collective-permute-done | bytes 1048608 | tf_op jit(solution)/shard_map/ppermute | solution.py:20
  52.5 0.0 collective-permute-start.1
  52.5 0.0 copy-done.2
  52.5 0.7 fusion.62
  53.1 3.7 %fusion.57 = (f32[]{:T(128)}, f32[]{:T(128)}, f32[]{:T(128)}, f32[]{:T(128)}, f32[]{:T(128)}) fusion(f32[4]{0:T(128)S(1)} %copy-done.4, s32[]{:T(128)} %bitcast.38, s32[]{:T(128)} %bitcast.22, s32[]{:T(128)} %bitcast.10, s32[]{:T(128)} %bitcast.9, s32[]{:T(128)} %bitcast.30), kind=kLoop, calls=%fused_computation.64 | loop fusion | flops 55 | bytes 56 | tf_op jit(solution)/shard_map/reduce_sum | solution.py:26
  62.0 0.0 copy-done.1
  62.0 0.4 select_reduce_fusion
  62.3 0.0 all-gather.2.cloned.1.call-done
  62.4 2.3 %fusion.8 = f32[512,256]{0,1:T(8,128)S(1)} fusion(bf16[256,2048]{1,0:T(8,128)(2,1)S(1)} %bitcast.140, bf16[1,512,2048]{2,1,0:T(8,128)(2,1)} %all-gather.2.cloned.1.call-done), kind=kOutput, calls=%fused_computation.11 | convolution fusion | flops 536870912 | bytes 3670016 | tf_op jit(solution)/shard_map/iap,jbp->iajb/dot_general | solution.py:63
  64.7 0.2 reshape.218
  64.9 1.0 copy.26
  65.9 3.5 %all-to-all-start.1 = ((f32[8,1,128,1,128]{4,2,3,1,0:T(8,128)}), f32[8,1,128,1,128]{4,2,3,1,0:T(8,128)S(1)}, u32[]{:S(2)}, u32[]{:S(2)}) async-start(f32[8,1,128,1,128]{4,2,3,1,0:T(8,128)} %bitcast.6), calls=%async_computation.1 | async-start | bytes 1048576 | tf_op jit(solution)/shard_map/all_to_all | solution.py:70
  69.4 8.6 %collective-permute-done.1 = bf16[1,256,2048]{2,1,0:T(8,128)(2,1)} collective-permute-done((bf16[1,256,2048]{2,1,0:T(8,128)(2,1)}, bf16[1,256,2048]{2,1,0:T(8,128)(2,1)}, u32[]{:S(2)}, u32[]{:S(2)}) %collective-permute-start.1) | collective-permute-done | bytes 1048608 | tf_op jit(solution)/shard_map/ppermute | solution.py:20
  78.0 0.0 collective-permute-start.2
  78.0 2.6 %fusion.14 = f32[512,256]{0,1:T(8,128)S(1)} fusion(bf16[1,512,2048]{2,1,0:T(8,128)(2,1)} %all-gather.2.cloned.1.call-done, bf16[1,256,2048]{2,1,0:T(8,128)(2,1)} %collective-permute-done.1), kind=kOutput, calls=%fused_computation.13 | convolution fusion | flops 536870912 | bytes 3670016 | tf_op jit(solution)/shard_map/iap,jbp->iajb/dot_general | solution.py:63
  80.7 0.2 reshape.231
  80.9 1.0 copy.32
  81.9 0.0 all-to-all-done.1
  81.9 4.2 %all-to-all-start.3 = ((f32[8,1,128,1,128]{4,2,3,1,0:T(8,128)}), f32[8,1,128,1,128]{4,2,3,1,0:T(8,128)}, u32[]{:S(2)}, u32[]{:S(2)}) async-start(f32[8,1,128,1,128]{4,2,3,1,0:T(8,128)} %bitcast.27), calls=%async_computation.3 | async-start | bytes 1048576 | tf_op jit(solution)/shard_map/all_to_all | solution.py:70
  86.1 0.2 select_reduce_fusion.1
  86.3 2.7 %fusion.11 = f32[512,256]{0,1:T(8,128)S(1)} fusion(bf16[1,512,2048]{2,1,0:T(8,128)(2,1)} %all-gather.2.cloned.1.call-done, bf16[1,256,2048]{2,1,0:T(8,128)(2,1)} %collective-permute-done), kind=kOutput, calls=%fused_computation.12 | convolution fusion | flops 536870912 | bytes 3670016 | tf_op jit(solution)/shard_map/iap,jbp->iajb/dot_general | solution.py:63
  89.0 1.0 reshape.226
  90.0 2.1 %copy.29 = f32[1,4,128,1,2,128]{5,2,1,4,3,0:T(8,128)} copy(f32[1,4,128,1,2,128]{2,1,5,4,3,0:T(4,128)} %reshape.226) | data formatting | bytes 1048576 | tf_op jit(solution)/shard_map/reshape | solution.py:66
  92.1 1.4 copy.28
  93.5 1.4 all-to-all-done.3
  94.9 4.1 %all-to-all-start.2 = ((f32[8,1,128,1,128]{4,2,3,1,0:T(8,128)}), f32[8,1,128,1,128]{4,2,3,1,0:T(8,128)}, u32[]{:S(2)}, u32[]{:S(2)}) async-start(f32[8,1,128,1,128]{4,2,3,1,0:T(8,128)} %bitcast.148), calls=%async_computation.2 | async-start | bytes 1048576 | tf_op jit(solution)/shard_map/all_to_all | solution.py:70
  99.1 2.8 %fusion.36 = f32[512,2048]{1,0:T(8,128)} fusion(bf16[256,2048]{1,0:T(8,128)(2,1)S(1)} %bitcast.141, f32[32,8,4,128]{3,2,1,0:T(4,128)S(1)} %bitcast.143, f32[512,256]{0,1:T(8,128)S(1)} %fusion.8, f32[256]{0:T(256)S(1)} %select_reduce_fusion.1, f32[512]{0:T(512)S(1)} %get-tuple-element.13), kind=kOutput, calls=%fused_computation.38 | convolution fusion | flops 537526272 | bytes 6294528 | tf_op jit(solution)/shard_map/iajb,jbp->iap/dot_general | solution.py:84
  101.9 1.4 copy.34
  103.2 0.0 collective-permute-done.2
  103.3 2.1 %fusion.17 = f32[512,256]{0,1:T(8,128)S(1)} fusion(bf16[1,512,2048]{2,1,0:T(8,128)(2,1)S(1)} %copy-done.5, bf16[1,256,2048]{2,1,0:T(8,128)(2,1)} %collective-permute-done.2), kind=kOutput, calls=%fused_computation.14 | convolution fusion | flops 536870912 | bytes 3670016 | tf_op jit(solution)/shard_map/iap,jbp->iajb/dot_general | solution.py:63
  105.4 0.2 reshape.236
  105.6 1.0 copy.35
  106.6 1.3 all-to-all-done.2
  107.9 3.5 %all-to-all-start.4 = ((f32[8,1,128,1,128]{4,2,3,1,0:T(8,128)}), f32[8,1,128,1,128]{4,2,3,1,0:T(8,128)S(1)}, u32[]{:S(2)}, u32[]{:S(2)}) async-start(f32[8,1,128,1,128]{4,2,3,1,0:T(8,128)} %bitcast.35), calls=%async_computation.4 | async-start | bytes 1048576 | tf_op jit(solution)/shard_map/all_to_all | solution.py:70
  111.4 0.0 reduce-scatter.2.cloned.1.call-start
  111.5 4.1 %fusion.22 = f32[512,2048]{1,0:T(8,128)} fusion(bf16[1,256,2048]{2,1,0:T(8,128)(2,1)} %collective-permute-done.1, f32[32,8,4,128]{3,2,1,0:T(4,128)S(1)} %bitcast.142, f32[512,256]{0,1:T(8,128)S(1)} %fusion.14, f32[512]{0:T(512)S(1)} %get-tuple-element.11, f32[256]{0:T(256)S(1)} %select_reduce_fusion.1), kind=kOutput, calls=%fused_computation.18 | convolution fusion | flops 537526272 | bytes 6294528 | tf_op jit(solution)/shard_map/iajb,jbp->iap/dot_general | solution.py:84
  115.5 1.4 copy.31
  116.9 4.1 %fusion.25 = f32[512,2048]{1,0:T(8,128)} fusion(bf16[1,256,2048]{2,1,0:T(8,128)(2,1)} %collective-permute-done, f32[32,8,4,128]{3,2,1,0:T(4,128)S(1)} %bitcast.144, f32[512,256]{0,1:T(8,128)S(1)} %fusion.11, f32[512]{0:T(512)S(1)} %get-tuple-element.12, f32[256]{0:T(256)S(1)} %select_reduce_fusion.1), kind=kOutput, calls=%fused_computation.21 | convolution fusion | flops 537526272 | bytes 6294528 | tf_op jit(solution)/shard_map/iajb,jbp->iap/dot_general | solution.py:84
  121.0 0.0 all-to-all-done.4
  121.0 0.3 copy.37
  121.3 7.9 %add_bitcast_fusion = f32[1,512,2048]{2,1,0:T(8,128)} fusion(f32[512,2048]{1,0:T(8,128)} %fusion.22, f32[512,2048]{1,0:T(8,128)} %fusion.36, f32[512,2048]{1,0:T(8,128)} %fusion.25, bf16[1,256,2048]{2,1,0:T(8,128)(2,1)} %collective-permute-done.2, f32[32,8,4,128]{3,2,1,0:T(4,128)S(1)} %bitcast.146, f32[512,256]{0,1:T(8,128)S(1)} %fusion.17, ...), kind=kOutput, calls=%fused_computation | convolution fusion | flops 540672000 | bytes 18877440 | tf_op jit(solution)/shard_map/iajb,jbp->iap/dot_general | solution.py:84
  129.2 0.0 reduce-scatter.2.cloned.1.call-update
  129.2 46.5 %reduce-scatter.2.cloned.1.call-done = f32[1,128,2048]{2,1,0:T(8,128)} async-done(((f32[1,512,2048]{2,1,0:T(8,128)}), f32[1,128,2048]{2,1,0:T(8,128)}) %reduce-scatter.2.cloned.1.call-update) | async-done | bytes 1048592 | tf_op jit(solution)/shard_map/reduce_scatter | solution.py:87
  (14 shorter events, 0.1 us)
Async XLA Ops:
  6.5 45.9 %copy-start.2 = (s32[4]{0:T(128)S(1)}, s32[4]{0:T(128)}, u32[]{:S(2)}) copy-start(s32[4]{0:T(128)} %param.8) | copy-start | bytes 52
  6.5 46.6 %copy-start.4 = (f32[4]{0:T(128)S(1)}, f32[4]{0:T(128)}, u32[]{:S(2)}) copy-start(f32[4]{0:T(128)} %param.6) | copy-start | bytes 52
  6.5 55.4 %copy-start.3 = (s32[1024]{0:T(1024)S(1)}, s32[1024]{0:T(1024)}, u32[]{:S(2)}) copy-start(s32[1024]{0:T(1024)} %param.9) | copy-start | bytes 12292
  6.5 55.4 %copy-start.1 = (f32[1024]{0:T(1024)S(1)}, f32[1024]{0:T(1024)}, u32[]{:S(2)}) copy-start(f32[1024]{0:T(1024)} %param.7) | copy-start | bytes 12292
  6.5 55.8 %all-gather.2.cloned.1.call-start = ((), (), s32[]{:S(2)}) async-start(), calls=%async_computation.6 | async-start | bytes 2621440 | tf_op jit(solution)/shard_map/all_gather | solution.py:56
  26.3 26.2 %collective-permute-start = (bf16[1,256,2048]{2,1,0:T(8,128)(2,1)S(1)}, bf16[1,256,2048]{2,1,0:T(8,128)(2,1)}, u32[]{:S(2)}, u32[]{:S(2)}) collective-permute-start(bf16[1,256,2048]{2,1,0:T(8,128)(2,1)S(1)} %bitcast.139), channel_id=1, source_target_pairs={{24,0},{0,8},{8,16},{16,24},{25,1},{1,9},{9,17},{17,25},{26,2},{2,... | collective-permute-start | bytes 3145736 | tf_op jit(solution)/shard_map/ppermute | solution.py:20
  52.5 25.5 %collective-permute-start.1 = (bf16[1,256,2048]{2,1,0:T(8,128)(2,1)}, bf16[1,256,2048]{2,1,0:T(8,128)(2,1)}, u32[]{:S(2)}, u32[]{:S(2)}) collective-permute-start(bf16[1,256,2048]{2,1,0:T(8,128)(2,1)} %collective-permute-done), channel_id=1, source_target_pairs={{24,0},{0,8},{8,16},{16,24},{25,1},{1,9},{9,17},{17,25},{26,2},{2,... | collective-permute-start | bytes 3145736 | tf_op jit(solution)/shard_map/ppermute | solution.py:20
  65.9 16.0 %all-to-all-start.1 = ((f32[8,1,128,1,128]{4,2,3,1,0:T(8,128)}), f32[8,1,128,1,128]{4,2,3,1,0:T(8,128)S(1)}, u32[]{:S(2)}, u32[]{:S(2)}) async-start(f32[8,1,128,1,128]{4,2,3,1,0:T(8,128)} %bitcast.6), calls=%async_computation.1 | async-start | bytes 1048576 | tf_op jit(solution)/shard_map/all_to_all | solution.py:70
  78.0 25.2 %collective-permute-start.2 = (bf16[1,256,2048]{2,1,0:T(8,128)(2,1)}, bf16[1,256,2048]{2,1,0:T(8,128)(2,1)}, u32[]{:S(2)}, u32[]{:S(2)}) collective-permute-start(bf16[1,256,2048]{2,1,0:T(8,128)(2,1)} %collective-permute-done.1), channel_id=1, source_target_pairs={{24,0},{0,8},{8,16},{16,24},{25,1},{1,9},{9,17},{17,25},{26,2},{2,... | collective-permute-start | bytes 3145736 | tf_op jit(solution)/shard_map/ppermute | solution.py:20
  81.9 7.1 %copy-start = (f32[8,1,128,1,128]{4,2,3,1,0:T(8,128)}, f32[8,1,128,1,128]{4,2,3,1,0:T(8,128)S(1)}, u32[]{:S(2)}) copy-start(f32[8,1,128,1,128]{4,2,3,1,0:T(8,128)S(1)} %all-to-all-done.1) | copy-start | bytes 1572868
  81.9 13.0 %all-to-all-start.3 = ((f32[8,1,128,1,128]{4,2,3,1,0:T(8,128)}), f32[8,1,128,1,128]{4,2,3,1,0:T(8,128)}, u32[]{:S(2)}, u32[]{:S(2)}) async-start(f32[8,1,128,1,128]{4,2,3,1,0:T(8,128)} %bitcast.27), calls=%async_computation.3 | async-start | bytes 1048576 | tf_op jit(solution)/shard_map/all_to_all | solution.py:70
  94.9 13.0 %all-to-all-start.2 = ((f32[8,1,128,1,128]{4,2,3,1,0:T(8,128)}), f32[8,1,128,1,128]{4,2,3,1,0:T(8,128)}, u32[]{:S(2)}, u32[]{:S(2)}) async-start(f32[8,1,128,1,128]{4,2,3,1,0:T(8,128)} %bitcast.148), calls=%async_computation.2 | async-start | bytes 1048576 | tf_op jit(solution)/shard_map/all_to_all | solution.py:70
  99.0 4.2 %copy-start.5 = (bf16[1,512,2048]{2,1,0:T(8,128)(2,1)S(1)}, bf16[1,512,2048]{2,1,0:T(8,128)(2,1)}, u32[]{:S(2)}) copy-start(bf16[1,512,2048]{2,1,0:T(8,128)(2,1)} %all-gather.2.cloned.1.call-done) | copy-start | bytes 6291460
  107.9 13.1 %all-to-all-start.4 = ((f32[8,1,128,1,128]{4,2,3,1,0:T(8,128)}), f32[8,1,128,1,128]{4,2,3,1,0:T(8,128)S(1)}, u32[]{:S(2)}, u32[]{:S(2)}) async-start(f32[8,1,128,1,128]{4,2,3,1,0:T(8,128)} %bitcast.35), calls=%async_computation.4 | async-start | bytes 1048576 | tf_op jit(solution)/shard_map/all_to_all | solution.py:70
  111.4 64.4 %reduce-scatter.2.cloned.1.call-start = ((), (), s32[]{:S(2)}) async-start(), calls=%async_computation.7 | async-start | bytes 5242880 | tf_op jit(solution)/shard_map/reduce_scatter | solution.py:87
Sparse Core Ops, SparseCore 0:
  8.9 25.2 all-gather.1
  129.3 46.3 reduce-scatter.1
